TPU v7x, 128 devices: a whole 4x4x4 slice. The times are simulated.
128 devices in a mesh: req: 8 (over x, core), exp: 16 (over y, z).
Axes of the slice: x: 4, y: 4, z: 4, core: 2. Of those that a mesh axis runs over, the one named last changes fastest.
Arguments:
- tokens: bfloat16 [16384, 2048], P(('req', 'exp')), may hold values from -6 to 6
- norm_gains: float32 [2, 2048], replicated, may hold values from 0.25 to 1.75
- w_query: bfloat16 [2048, 4, 2048], P(None, None, 'exp'), may hold values from -0.125 to 0.125
- w_keyval: bfloat16 [2048, 2, 2048], P(None, None, 'exp'), may hold values from -0.125 to 0.125
- w_out: bfloat16 [4, 2048, 2048], P(None, 'exp'), may hold values from -0.125 to 0.125
- page_pool: bfloat16 [32, 128, 16, 256], P('req', None, 'exp'), may hold values from -3000 to 3000
- page_dest: int32 [32], replicated, may hold values from 0 to 31, as said below
- prompt_lens: int32 [8, 4], P('req'), may hold values from 1 to 1024, 2048 in all within a row
- att_ids: int32 [16384, 2], P('req'), may hold values from 0 to 3, all different within a row
- att_gates: float32 [16384, 2], P('req'), may hold values from 0.1 to 1
- w_in: bfloat16 [2048, 2, 22528], P(None, None, 'exp'), may hold values from -0.125 to 0.125
- w_down: bfloat16 [22528, 2048], P('exp'), may hold values from -0.109375 to 0.109375
- moe_ids: int32 [16384, 2], P(('req', 'exp')), may hold values from 0 to 7, all different within a row; in each aligned block of 128 rows (0 to 127, 128 to 255, ...) at most 40 rows name the same one
- moe_gates: float32 [16384, 2], P(('req', 'exp')), may hold values from 0.1 to 1
- adapters: bfloat16 [64, 2, 16, 2048], P('exp'), may hold values from -0.25 to 0.25
- req_adapter: int32 [32], replicated, may hold values from 0 to 63, as said below
Outputs:
- layer_out: bfloat16 [16384, 2048], P(('req', 'exp'))
Inputs may be any that keep to these rules, and one draw needn't show every extreme that they name: `page_dest`: pool slot g * 4 + p holds the pages of request ((g + s_p) mod the number of groups) * 4 + p, where the 4 shifts s_p are distinct: a group's slots go to 4 different groups, and each group receives one request a slot. `prompt_lens`: the 4 lengths of a group sum to 2048. `att_ids`: the two ids of a token differ. `moe_ids`: the two ids of a token differ; among the 128 tokens of one device no expert is named by more than 40, a bound that some block reaches. `req_adapter`: exactly 16 distinct adapters are named, adapters 0 and 63 among them.
All inputs are finite; a program needn't handle non-finite values.
Results may differ from a plain program's by a relative error of at most 0.015.
Values may be sent and summed in bfloat16 or wider, within the bound.
A program may use at most 192 MiB of HBM per device.

v0:
```python
import math
import jax
import jax.numpy as jnp
from jax import lax
from jax.sharding import PartitionSpec as P

HD = 128
AEXP = 4
EXPERTS = 8
CACHE = 128
CAP = 40
norm_eps = 1e-05


def rms_scale(values, gain):
    values = values.astype(jnp.float32)
    factor = lax.rsqrt(jnp.mean(values * values, axis=-1, keepdims=True) + norm_eps)
    return (values * factor * gain).astype(jnp.bfloat16)


def rotate(vectors, places):
    half_width = vectors.shape[-1] // 2
    steps_idx = jnp.arange(half_width, dtype=jnp.float32)
    inverse = jnp.power(10000.0, steps_idx * (-2.0 / vectors.shape[-1]))
    angles = places.astype(jnp.float32)[:, None] * inverse[None, :]
    angles = angles.reshape((places.shape[0],) + (1,) * (vectors.ndim - 2) + (half_width,))
    cosine = jnp.cos(angles)
    sine_part = jnp.sin(angles)
    former = vectors[..., :half_width]
    latter = vectors[..., half_width:]
    return jnp.concatenate(
        [former * cosine - latter * sine_part, former * sine_part + latter * cosine], axis=-1
    )


def group_positions(lengths, total, cached):
    finish = jnp.cumsum(lengths)
    beginning = finish - lengths
    indices = jnp.arange(total, dtype=jnp.int32)
    segment = jnp.sum((indices[:, None] >= finish[None, :]).astype(jnp.int32), axis=1)
    member = segment[:, None] == jnp.arange(lengths.shape[0], dtype=jnp.int32)[None, :]
    offset = jnp.sum(jnp.where(member, beginning[None, :], 0), axis=1)
    return (segment, cached + indices - offset)


def attend_block(queries, key_rows, val_rows, visible, scale_factor):
    scores = (
        jnp.einsum("qhd,khd->hqk", queries, key_rows, preferred_element_type=jnp.float32)
        * scale_factor
    )
    scores = jnp.where(visible[None, :, :], scores, -1e30)
    highest = jnp.max(scores, axis=-1, keepdims=True)
    raised = jnp.exp(scores - highest)
    weights = (raised / jnp.sum(raised, axis=-1, keepdims=True)).astype(jnp.bfloat16)
    return jnp.einsum("hqk,khd->qhd", weights, val_rows, preferred_element_type=jnp.float32).astype(
        jnp.bfloat16
    )


def on_device(
    tokens,
    norm_gains,
    w_query,
    w_keyval,
    w_out,
    page_pool,
    page_dest,
    prompt_lens,
    att_ids,
    att_gates,
    w_in,
    w_down,
    moe_ids,
    moe_gates,
    adapters,
    req_adapter,
):
    groups = lax.axis_size("req")
    columns = lax.axis_size("exp")
    group_index = lax.axis_index("req")
    column_index = lax.axis_index("exp")
    tok_rows = tokens.shape[0]
    width = tokens.shape[1]
    group_rows = tok_rows * columns
    local_heads = w_query.shape[2] // HD
    slot_count = page_pool.shape[0]
    group_numbers = jnp.arange(groups, dtype=jnp.int32)
    own_target = (
        lax.dynamic_slice_in_dim(page_dest, group_index * slot_count, slot_count) // slot_count
    )
    outgoing_map = (own_target[None, :] == group_numbers[:, None]).astype(jnp.bfloat16)
    outgoing = jnp.dot(
        outgoing_map, page_pool.reshape(slot_count, -1), preferred_element_type=jnp.float32
    )
    outgoing = outgoing.astype(jnp.bfloat16).reshape((groups,) + page_pool.shape[1:])
    incoming = lax.all_to_all(outgoing, "req", split_axis=0, concat_axis=0, tiled=True)
    pool_slots = jnp.arange(page_dest.shape[0], dtype=jnp.int32)
    wanted = group_index * slot_count + jnp.arange(slot_count, dtype=jnp.int32)
    sender = (
        jnp.sum(jnp.where(page_dest[None, :] == wanted[:, None], pool_slots[None, :], 0), axis=1)
        // slot_count
    )
    incoming_map = (sender[:, None] == group_numbers[None, :]).astype(jnp.bfloat16)
    cached = jnp.dot(incoming_map, incoming.reshape(groups, -1), preferred_element_type=jnp.float32)
    cached = cached.astype(jnp.bfloat16).reshape(page_pool.shape)
    segment, places = group_positions(prompt_lens.reshape(-1), group_rows, CACHE)
    normed = rms_scale(tokens, norm_gains[0])
    gathered, factor_table = (
        lax.all_gather(normed, "exp", axis=0, tiled=True),
        lax.all_gather(adapters, "exp", axis=0, tiled=True),
    )
    queries = jnp.dot(gathered, w_query.reshape(width, -1), preferred_element_type=jnp.float32)
    queries = rotate(queries.reshape(group_rows, AEXP, local_heads, HD), places).astype(
        jnp.bfloat16
    )
    chosen_rows = (jnp.arange(group_rows, dtype=jnp.int32)[:, None] * AEXP + att_ids).reshape(-1)
    chosen = jnp.take(queries.reshape(group_rows * AEXP, local_heads * HD), chosen_rows, axis=0)
    keyval = jnp.dot(gathered, w_keyval.reshape(width, -1), preferred_element_type=jnp.float32)
    keyval = keyval.reshape(group_rows, 2, local_heads, HD)
    new_keys = rotate(keyval[:, 0], places).astype(jnp.bfloat16)
    new_values = keyval[:, 1].astype(jnp.bfloat16)
    key_rows = jnp.concatenate([cached[..., :HD].reshape(-1, local_heads, HD), new_keys], axis=0)
    val_rows = jnp.concatenate([cached[..., HD:].reshape(-1, local_heads, HD), new_values], axis=0)
    key_segment = jnp.concatenate(
        [jnp.repeat(jnp.arange(slot_count, dtype=jnp.int32), CACHE), segment]
    )
    key_index = jnp.concatenate(
        [jnp.full((slot_count * CACHE,), -1, jnp.int32), jnp.arange(group_rows, dtype=jnp.int32)]
    )
    query_total = 2 * group_rows
    block_rows = 1024
    block_count = query_total // block_rows
    query_segment = jnp.repeat(segment, 2).reshape(block_count, block_rows)
    query_index = jnp.repeat(jnp.arange(group_rows, dtype=jnp.int32), 2).reshape(
        block_count, block_rows
    )
    scale_factor = 1.0 / math.sqrt(HD)

    def block_step(items):
        block_queries, block_segment, block_index = items
        visible = (block_segment[:, None] == key_segment[None, :]) & (
            key_index[None, :] <= block_index[:, None]
        )
        return attend_block(block_queries, key_rows, val_rows, visible, scale_factor)

    heads_out = lax.map(
        block_step,
        (chosen.reshape(block_count, block_rows, local_heads, HD), query_segment, query_index),
    )
    heads_out = heads_out.reshape(group_rows, 2, local_heads * HD)
    slot_weights = jnp.where(
        att_ids[:, :, None] == jnp.arange(AEXP, dtype=jnp.int32)[None, None, :],
        att_gates[:, :, None],
        0.0,
    )
    mixed = jnp.einsum(
        "tje,tjx->tex", slot_weights, heads_out.astype(jnp.float32), precision=lax.Precision.HIGHEST
    ).astype(jnp.bfloat16)
    flat_mixed = mixed.reshape(group_rows, -1)
    flat_out = w_out.reshape(-1, width)
    attended = lax.psum_scatter(
        jnp.dot(flat_mixed, flat_out, preferred_element_type=jnp.float32).astype(jnp.bfloat16),
        "exp",
        scatter_dimension=0,
        tiled=True,
    ).astype(jnp.float32)
    hidden_state = (tokens.astype(jnp.float32) + attended).astype(jnp.bfloat16)
    hnorm = rms_scale(hidden_state, norm_gains[1])
    expert_flat = moe_ids.reshape(-1)
    expert_hits = (expert_flat[:, None] == jnp.arange(EXPERTS, dtype=jnp.int32)[None, :]).astype(
        jnp.int32
    )
    earlier = jnp.cumsum(expert_hits, axis=0) - expert_hits
    route_slot = jnp.sum(earlier * expert_hits, axis=1) + expert_flat * CAP
    table_size = EXPERTS * CAP
    placing = (jnp.arange(table_size, dtype=jnp.int32)[:, None] == route_slot[None, :]).reshape(
        table_size, tok_rows, 2
    )
    placing = jnp.any(placing, axis=2).astype(jnp.bfloat16)
    packed = jnp.dot(placing, hnorm, preferred_element_type=jnp.float32).astype(jnp.bfloat16)
    packed = packed.reshape(EXPERTS, CAP, width)
    copies = columns // EXPERTS
    spread_rows = jnp.repeat(packed, copies, axis=0)
    arrived = lax.all_to_all(spread_rows, "exp", split_axis=0, concat_axis=0, tiled=True)
    flat_rows = arrived.reshape(-1, width)
    gate_up = jnp.einsum("nd,dkf->nkf", flat_rows, w_in, preferred_element_type=jnp.float32)
    inner_act = (jax.nn.silu(gate_up[:, 0]) * gate_up[:, 1]).astype(jnp.bfloat16)
    partial_out = jnp.dot(inner_act, w_down, preferred_element_type=jnp.float32).reshape(
        columns, CAP, width
    )
    returned = lax.all_to_all(
        partial_out.astype(jnp.bfloat16), "exp", split_axis=0, concat_axis=0, tiled=True
    ).astype(partial_out.dtype)
    summed = jnp.sum(returned.reshape(EXPERTS, copies, CAP, width), axis=1).reshape(
        table_size, width
    )
    routed_rows = jnp.take(summed, route_slot, axis=0).reshape(tok_rows, 2, width)
    expert_out = jnp.sum(routed_rows * moe_gates[:, :, None], axis=1)
    own_segment = lax.dynamic_slice_in_dim(segment, column_index * tok_rows, tok_rows)
    wanted_ids = lax.dynamic_slice_in_dim(req_adapter, group_index * slot_count, slot_count)
    group_factors = jnp.take(factor_table, wanted_ids, axis=0)
    lowrank = jnp.einsum(
        "td,qrd->tqr", hnorm, group_factors[:, 0], preferred_element_type=jnp.float32
    )
    member = own_segment[:, None] == jnp.arange(slot_count, dtype=jnp.int32)[None, :]
    lowrank = jnp.where(member[:, :, None], lowrank, 0.0).astype(jnp.bfloat16)
    delta = jnp.einsum(
        "tqr,qrd->td", lowrank, group_factors[:, 1], preferred_element_type=jnp.float32
    )
    return (hidden_state.astype(jnp.float32) + expert_out + delta).astype(jnp.bfloat16)


def solution(mesh):
    in_specs = (
        P(("req", "exp"), None),
        P(),
        P(None, None, "exp"),
        P(None, None, "exp"),
        P(None, "exp", None),
        P("req", None, "exp", None),
        P(),
        P("req", None),
        P("req", None),
        P("req", None),
        P(None, None, "exp"),
        P("exp", None),
        P(("req", "exp"), None),
        P(("req", "exp"), None),
        P("exp", None, None, None),
        P(),
    )
    out_specs = P(("req", "exp"), None)
    return jax.shard_map(
        on_device, mesh=mesh, in_specs=in_specs, out_specs=out_specs, check_vma=False
    )
```

profile of v0, /device:TPU:16, one launch (start us, length us, event | category | flops | bytes accessed | tf_op | source)
XLA Modules:
  0.0 430.3 jit_solution(572273095030612041)
XLA Ops:
  13.8 4.4 %all-to-all-start = ((bf16[8,128,1,256]{3,1,2,0:T(8,128)(2,1)}), bf16[8,128,1,256]{3,1,2,0:T(8,128)(2,1)}, u32[]{:S(2)}, u32[]{:S(2)}) async-start(bf16[8,128,1,256]{3,1,2,0:T(8,128)(2,1)} %copy.128), calls=%async_computation | async-start | bytes 1048576 | tf_op jit(solution)/shard_map/all_to_all | solution.py:96
  21.5 3.3 copy.159
  24.8 4.3 copy.123
  42.1 42.5 %all-gather.3.cloned.1.call-done = bf16[2048,2048]{1,0:T(8,128)(2,1)} async-done(((bf16[128,2048]{1,0:T(8,128)(2,1)}), bf16[2048,2048]{1,0:T(8,128)(2,1)}) %all-gather.3.cloned.1.call-update) | async-done | bytes 8388624 | tf_op jit(solution)/shard_map/all_gather | solution.py:109
  84.6 5.9 %fusion.24 = f32[2048,2,1,128]{0,3,1,2:T(8,128)S(1)} fusion(bf16[2,128,2048]{2,1,0:T(8,128)(2,1)S(1)} %bitcast.178, bf16[2048,2048]{1,0:T(8,128)(2,1)} %all-gather.3.cloned.1.call-done), kind=kOutput, calls=%fused_computation.34 | convolution fusion | flops 2147483648 | bytes 11534336 | tf_op jit(solution)/shard_map/dot_general | solution.py:118
  92.5 4.5 %fusion.18 = f32[2048,4,1,128]{0,3,1,2:T(8,128)S(1)} fusion(bf16[4,128,2048]{2,1,0:T(8,128)(2,1)S(1)} %bitcast.173, bf16[2048,2048]{1,0:T(8,128)(2,1)S(1)} %copy-done.22), kind=kOutput, calls=%fused_computation.32 | convolution fusion | flops 4294967296 | bytes 14680064 | tf_op jit(solution)/shard_map/dot_general | solution.py:112
  98.8 4.1 copy.124
  105.3 4.3 %fusion.49 = (bf16[2048,1,64]{0,2,1:T(8,128)(2,1)S(1)}, bf16[2048,1,64]{0,2,1:T(8,128)(2,1)S(1)}) fusion(f32[2048,1,128]{0,2,1:T(8,128)} %slice_bitcast_fusion, f32[64]{0:T(128)} %copy-done.19, f32[2048]{0:T(1024)} %copy-done.11), kind=kLoop, calls=%fused_computation.81 | loop fusion | flops 1179648 | bytes 1581312 | tf_op jit(solution)/shard_map/convert.2
  111.9 4.7 %pad_maximum_fusion = bf16[8192,128]{1,0:T(8,128)(2,1)} fusion(bf16[8192,64]{1,0:T(8,128)(2,1)} %bitcast.164, bf16[8192,64]{1,0:T(8,128)(2,1)} %bitcast.163), kind=kLoop, calls=%fused_computation.40 | loop fusion | flops 4194304 | bytes 4194304 | tf_op jit(solution)/shard_map/concatenate | solution.py:31
  116.6 12.9 %gather_fusion = bf16[4096,128]{1,0:T(8,128)(2,1)S(1)} fusion(bf16[8192,128]{1,0:T(8,128)(2,1)} %pad_maximum_fusion, s32[4096]{0:T(1024)S(1)} %copy-done.14), kind=kCustom, calls=%fused_computation | custom fusion | bytes 2113536 | tf_op jit(solution)/shard_map/jit(_take)/gather | solution.py:117
  131.7 36.9 %while.11 = (s32[]{:T(128)}, bf16[4,1024,1,128]{3,1,2,0:T(8,128)(2,1)}, s32[4,1024]{1,0:T(4,128)}, s32[2560]{0:T(1024)S(1)}, s32[4,1024]{1,0:T(4,128)S(1)}, /*in...) while((s32[]{:T(128)}, ...), condition=%wide.region_8.9_spmd, body=%wide.region_5.8_spmd.sunk | while | flops 1371142144 | bytes 35980420 | solution.py:146
  132.6 4.0 fusion.96
  138.2 2.9 fusion.98
  141.8 4.0 fusion.96
  147.4 2.9 fusion.98
  151.0 4.0 fusion.96
  156.6 2.9 fusion.98
  160.2 4.0 fusion.96
  168.7 14.3 %fusion.31 = bf16[2048,4,128]{2,1,0:T(4,128)(2,1)S(1)} fusion(bf16[2048,2,128]{2,1,0:T(2,128)(2,1)} %bitcast.33, f32[2048,2]{1,0:T(8,128)} %copy.120, s32[2048,2]{1,0:T(8,128)S(1)} %copy-done.7), kind=kOutput, calls=%fused_computation.46 | convolution fusion | flops 26247168 | bytes 3178496 | tf_op jit(solution)/shard_map/tje,tjx->tex/dot_general | solution.py:156
  183.0 6.5 %bitcast_convert_fusion = bf16[2048,2048]{1,0:T(8,128)(2,1)} fusion(bf16[4,128,2048]{2,1,0:T(8,128)(2,1)S(1)} %copy-done, bf16[2048,4,128]{2,1,0:T(4,128)(2,1)S(1)} %fusion.31), kind=kOutput, calls=%fused_computation.20 | convolution fusion | flops 4299161600 | bytes 12582912 | tf_op jit(solution)/shard_map/dot_general | solution.py:162
  191.9 83.4 %reduce-scatter.2.cloned.1.call-done = bf16[128,2048]{1,0:T(8,128)(2,1)} async-done(((bf16[2048,2048]{1,0:T(8,128)(2,1)}), bf16[128,2048]{1,0:T(8,128)(2,1)}) %reduce-scatter.2.cloned.1.call-update) | async-done | bytes 524304 | tf_op jit(solution)/shard_map/reduce_scatter | solution.py:161
  278.6 44.5 %all_to_all.15 = bf16[16,40,2048]{2,1,0:T(8,128)(2,1)S(1)} all-to-all(bf16[16,40,2048]{2,1,0:T(8,128)(2,1)S(1)} %bitcast.162), channel_id=1, replica_groups=mesh['req'=8,'exp'=16] {'exp'}, dimensions={0} | all-to-all | bytes 5242880 | tf_op jit(solution)/shard_map/all_to_all | solution.py:184
  323.2 11.9 %fusion.10 = f32[640,2,1408]{2,0,1:T(8,128)S(1)} fusion(bf16[640,2048,1]{1,0,2:T(8,128)(2,1)S(1)} %bitcast.171, bf16[2048,2,1408]{2,1,0:T(2,128)(2,1)} %param.28), kind=kOutput, calls=%fused_computation.21 | convolution fusion | flops 7381975040 | bytes 21364736 | tf_op jit(solution)/shard_map/nd,dkf->nkf/dot_general | solution.py:186
  335.6 6.1 %fusion.21 = bf16[16,40,2048]{2,1,0:T(8,128)(2,1)} fusion(bf16[1408,2048]{1,0:T(8,128)(2,1)S(1)} %bitcast.195, f32[16,40,1408]{2,1,0:T(8,128)S(1)} %bitcast.170, f32[16,40,1408]{2,1,0:T(8,128)S(1)} %bitcast.169), kind=kOutput, calls=%fused_computation.33 | convolution fusion | flops 3697704960 | bytes 15597568 | tf_op jit(solution)/shard_map/dot_general | solution.py:188
  341.7 7.0 %all-to-all-start.2 = ((bf16[16,40,2048]{2,1,0:T(8,128)(2,1)}), bf16[16,40,2048]{2,1,0:T(8,128)(2,1)}, u32[]{:S(2)}, u32[]{:S(2)}) async-start(bf16[16,40,2048]{2,1,0:T(8,128)(2,1)} %fusion.21), calls=%async_computation.3 | async-start | bytes 5242880 | tf_op jit(solution)/shard_map/all_to_all | solution.py:191
  350.1 45.9 %all-gather.5.cloned.1.call-done = bf16[64,2,16,2048]{3,2,1,0:T(8,128)(2,1)} async-done(((bf16[4,2,16,2048]{3,2,1,0:T(8,128)(2,1)}), bf16[64,2,16,2048]{3,2,1,0:T(8,128)(2,1)}) %all-gather.5.cloned.1.call-update) | async-done | bytes 8388624 | tf_op jit(solution)/shard_map/all_gather | solution.py:110
  395.9 4.0 gather_fusion.2
  400.8 4.1 convert_reduce_fusion
  404.9 5.3 %gather_fusion.1 = f32[256,2048]{1,0:T(8,128)} fusion(f32[320,2048]{1,0:T(8,128)} %bitcast.161, s32[1024]{0:T(1024)S(1)} %pad_clamp_fusion.1), kind=kCustom, calls=%fused_computation.1 | custom fusion | bytes 4195328 | tf_op jit(solution)/shard_map/jit(_take)/gather | solution.py:197
  410.3 3.5 gather.19
  413.8 6.6 %multiply_reduce_fusion = f32[128,2048]{1,0:T(8,128)} fusion(f32[128,2,2048]{2,1,0:T(2,128)} %gather.19, pred[128,2]{1,0:T(8,128)(4,1)S(1)} %copy.139, f32[128,2]{1,0:T(8,128)S(1)} %copy.142), kind=kLoop, calls=%fused_computation.42 | loop fusion | flops 1310720 | bytes 3147008 | tf_op jit(solution)/shard_map/reduce_sum | solution.py:198
  420.4 3.1 fusion.28
  (164 shorter events, 54.4 us)
Async XLA Ops:
  6.5 176.4 %copy-start = (bf16[4,128,2048]{2,1,0:T(8,128)(2,1)S(1)}, bf16[4,128,2048]{2,1,0:T(8,128)(2,1)}, u32[]{:S(2)}) copy-start(bf16[4,128,2048]{2,1,0:T(8,128)(2,1)} %param.22) | copy-start | bytes 6291460
  6.5 6.0 %copy-start.23 = (s32[32]{0:T(128)S(1)}, s32[32]{0:T(128)}, u32[]{:S(2)}) copy-start(s32[32]{0:T(128)} %param.24) | copy-start | bytes 388
  6.5 78.1 %all-gather.3.cloned.1.call-start = ((), (), s32[]{:S(2)}) async-start(), calls=%async_computation.4 | async-start | bytes 8912896 | tf_op jit(solution)/shard_map/all_gather | solution.py:109
  9.3 9.0 %copy-start.13 = (s32[2048,2]{0,1:T(2,128)S(1)}, s32[2048,2]{0,1:T(2,128)}, u32[]{:S(2)}) copy-start(s32[2048,2]{0,1:T(2,128)} %param.26) | copy-start | bytes 49156
  13.8 7.5 %copy-start.24 = (s32[1,4]{1,0:T(1,128)S(1)}, s32[1,4]{1,0:T(1,128)}, u32[]{:S(2)}) copy-start(s32[1,4]{1,0:T(1,128)} %param.25) | copy-start | bytes 52
  13.8 26.3 %all-to-all-start = ((bf16[8,128,1,256]{3,1,2,0:T(8,128)(2,1)}), bf16[8,128,1,256]{3,1,2,0:T(8,128)(2,1)}, u32[]{:S(2)}, u32[]{:S(2)}) async-start(bf16[8,128,1,256]{3,1,2,0:T(8,128)(2,1)} %copy.128), calls=%async_computation | async-start | bytes 1048576 | tf_op jit(solution)/shard_map/all_to_all | solution.py:96
  18.2 257.1 %reduce-scatter.2.cloned.1.call-start = ((), (), s32[]{:S(2)}) async-start(), calls=%async_computation.5 | async-start | bytes 8912896 | tf_op jit(solution)/shard_map/reduce_scatter | solution.py:161
  30.4 3.3 copy-start.15
  32.0 8.1 %copy-start.10 = (s32[2048]{0:T(1024)}, s32[2048]{0:T(1024)S(1)}, u32[]{:S(2)}) copy-start(s32[2048]{0:T(1024)S(1)} %convert_reduce_fusion.1) | copy-start | bytes 24580
  33.7 50.9 %copy-start.8 = (bf16[256,2048]{1,0:T(8,128)(2,1)S(1)}, bf16[256,2048]{1,0:T(8,128)(2,1)}, u32[]{:S(2)}) copy-start(bf16[256,2048]{1,0:T(8,128)(2,1)} %copy.130) | copy-start | bytes 3145732
  35.1 6.7 %copy-start.19 = (f32[64]{0:T(128)}, f32[64]{0:T(128)S(1)}, u32[]{:S(2)}) copy-start(f32[64]{0:T(128)S(1)} %multiply_power_fusion) | copy-start | bytes 772
  36.0 5.8 %copy-start.11 = (f32[2048]{0:T(1024)}, f32[2048]{0:T(1024)S(1)}, u32[]{:S(2)}) copy-start(f32[2048]{0:T(1024)S(1)} %subtract_convert_fusion.1) | copy-start | bytes 24580
  84.6 7.8 %copy-start.22 = (bf16[2048,2048]{1,0:T(8,128)(2,1)S(1)}, bf16[2048,2048]{1,0:T(8,128)(2,1)}, u32[]{:S(2)}) copy-start(bf16[2048,2048]{1,0:T(8,128)(2,1)} %all-gather.3.cloned.1.call-done) | copy-start | bytes 25165828
  90.5 2.0 copy-start.5
  92.5 4.5 %copy-start.3 = (f32[2048,64]{0,1:T(8,128)S(1)}, f32[2048,64]{0,1:T(8,128)}, u32[]{:S(2)}) copy-start(f32[2048,64]{0,1:T(8,128)} %get-tuple-element.159) | copy-start | bytes 1572868
  92.5 4.5 %copy-start.4 = (f32[2048,64]{0,1:T(8,128)S(1)}, f32[2048,64]{0,1:T(8,128)}, u32[]{:S(2)}) copy-start(f32[2048,64]{0,1:T(8,128)} %get-tuple-element.160) | copy-start | bytes 1572868
  105.3 5.5 %copy-start.6 = (bf16[2048,1,128]{0,2,1:T(8,128)(2,1)S(1)}, bf16[2048,1,128]{0,2,1:T(8,128)(2,1)}, u32[]{:S(2)}) copy-start(bf16[2048,1,128]{0,2,1:T(8,128)(2,1)} %fusion.52) | copy-start | bytes 1572868
  111.9 4.7 %copy-start.14 = (s32[4096]{0:T(1024)S(1)}, s32[4096]{0:T(1024)}, u32[]{:S(2)}) copy-start(s32[4096]{0:T(1024)} %broadcast_clamp_fusion) | copy-start | bytes 49156
  116.6 13.0 %copy-start.16 = (pred[4,1024]{1,0:T(4,128)(4,1)S(1)}, pred[4,1024]{1,0:T(4,128)(4,1)}, u32[]{:S(2)}) copy-start(pred[4,1024]{1,0:T(4,128)(4,1)} %compare_and_fusion) | copy-start | bytes 12292
  116.6 15.1 %copy-start.17 = (s32[2560]{0:T(1024)S(1)}, s32[2560]{0:T(1024)}, u32[]{:S(2)}) copy-start(s32[2560]{0:T(1024)} %pad_add_fusion) | copy-start | bytes 30724
  116.6 15.1 %copy-start.25 = (s32[2560]{0:T(1024)S(1)}, s32[2560]{0:T(1024)}, u32[]{:S(2)}) copy-start(s32[2560]{0:T(1024)} %constant.115.clone.1) | copy-start | bytes 30724
  131.7 36.9 %copy-start.7 = (s32[2048,2]{1,0:T(8,128)S(1)}, s32[2048,2]{1,0:T(8,128)}, u32[]{:S(2)}) copy-start(s32[2048,2]{1,0:T(8,128)} %copy.119) | copy-start | bytes 49156
  136.6 1.6 copy-start.9
  189.5 85.8 %copy-start.1 = (bf16[128,2048]{1,0:T(8,128)(2,1)S(1)}, bf16[128,2048]{1,0:T(8,128)(2,1)}, u32[]{:S(2)}) copy-start(bf16[128,2048]{1,0:T(8,128)(2,1)} %param.18) | copy-start | bytes 1572868
  189.5 87.2 %copy-start.12 = (f32[1,2048]{1,0:T(1,128)S(1)}, f32[1,2048]{1,0:T(1,128)}, u32[]{:S(2)}) copy-start(f32[1,2048]{1,0:T(1,128)} %get-tuple-element.158) | copy-start | bytes 24580
  189.5 206.4 %all-gather.5.cloned.1.call-start = ((), (), s32[]{:S(2)}) async-start(), calls=%async_computation.6 | async-start | bytes 8912896 | tf_op jit(solution)/shard_map/all_gather | solution.py:110
  278.6 57.0 %slice-start = ((s8[5767168]{0:T(1024)(128)(4,1)}), s8[4194304]{0:T(1024)(128)(4,1)S(1)}, s32[]{:S(2)}) async-start(s8[5767168]{0:T(1024)(128)(4,1)} %bitcast.194), calls=%async_computation.7 | async-start | bytes 8388608
  323.2 12.4 %slice-start.1 = ((s8[5767168]{0:T(1024)(128)(4,1)}), s8[1572864]{0:T(1024)(128)(4,1)S(1)}, s32[]{:S(2)}) async-start(s8[5767168]{0:T(1024)(128)(4,1)} %bitcast.194), calls=%async_computation.8 | async-start | bytes 3145728
  341.7 7.4 %copy-start.20 = (f32[128,2]{0,1:T(2,128)S(1)}, f32[128,2]{0,1:T(2,128)}, u32[]{:S(2)}) copy-start(f32[128,2]{0,1:T(2,128)} %param.31) | copy-start | bytes 3076
  341.7 8.3 %copy-start.21 = (s32[32]{0:T(128)S(1)}, s32[32]{0:T(128)}, u32[]{:S(2)}) copy-start(s32[32]{0:T(128)} %param.33) | copy-start | bytes 388
  341.7 59.1 %all-to-all-start.2 = ((bf16[16,40,2048]{2,1,0:T(8,128)(2,1)}), bf16[16,40,2048]{2,1,0:T(8,128)(2,1)}, u32[]{:S(2)}, u32[]{:S(2)}) async-start(bf16[16,40,2048]{2,1,0:T(8,128)(2,1)} %fusion.21), calls=%async_computation.3 | async-start | bytes 5242880 | tf_op jit(solution)/shard_map/all_to_all | solution.py:191
  413.8 6.6 %copy-start.2 = (bf16[128,2048]{1,0:T(8,128)(2,1)S(1)}, bf16[128,2048]{1,0:T(8,128)(2,1)}, u32[]{:S(2)}) copy-start(bf16[128,2048]{1,0:T(8,128)(2,1)} %reduce-scatter.2.cloned.1.call-done) | copy-start | bytes 1572868
  (4 other events, 5.5 us)
Sparse Core Ops, SparseCore 0:
  11.5 73.1 all-gather.2
  189.7 85.6 reduce-scatter.1
  277.5 118.3 all-gather.4
where the time goes:
time: 435 us; the launch traced here: 430 us
  waiting for transfers between devices  173 us (40%)
  matrix products  82.2 us (19%)
  local copies, waits for them, and re-layouts  64 us (15%)
  blocking collectives  44.5 us (10%)
  other arithmetic  41.6 us (10%)
  between operations  13.9 us (3%)
  starting transfers between devices  11.5 us (3%)
    reduce_scatter x1, waiting for transfers between devices, on_device(): lax.psum_scatter(jnp.dot(flat_mixed, flat_out, preferred_element_type=jnp...  83.4 us
    all_gather x1, waiting for transfers between devices, on_device(): lax.all_gather(adapters, 'exp', axis=0, tiled=True)  45.9 us
    all_to_all x1, blocking collectives, on_device(): lax.all_to_all(spread_rows, 'exp', split_axis=0, concat_axis=0, tiled=True)  44.5 us
    all_gather x1, waiting for transfers between devices, on_device(): lax.all_gather(normed, 'exp', axis=0, tiled=True)  42.5 us
    dot_general x4, matrix products, attend_block(): jnp.einsum('qhd,khd->hqk', queries, key_rows, preferred_element_type=jnp....  16.1 us
    dot_general x1, matrix products, on_device(): jnp.einsum('tje,tjx->tex', slot_weights, heads_out.astype(jnp.float32), p...  14.3 us
    gather x1, local copies, waits for them, and re-layouts, on_device(): jnp.take(queries.reshape(group_rows * AEXP, local_heads * HD), chosen_row...  12.9 us
    dot_general x1, matrix products, on_device(): jnp.einsum('nd,dkf->nkf', flat_rows, w_in, preferred_element_type=jnp.flo...  11.9 us
  transfers between devices with their start and end apart: 5, of which 3 were waited for; matrix products, arithmetic and copies ran while one was open for 13% of the time, Pallas kernels for 0%

commit v1 on v0

--- a/solution.py
+++ b/solution.py
@@ -107,7 +107,9 @@
     normed = rms_scale(tokens, norm_gains[0])
     gathered, factor_table = (
         lax.all_gather(normed, "exp", axis=0, tiled=True),
-        lax.all_gather(adapters, "exp", axis=0, tiled=True),
+        jnp.concatenate(
+            lax.all_to_all(jnp.stack([adapters] * lax.axis_size("exp")), "exp", 0, 0), axis=0
+        ),
     )
     queries = jnp.dot(gathered, w_query.reshape(width, -1), preferred_element_type=jnp.float32)
     queries = rotate(queries.reshape(group_rows, AEXP, local_heads, HD), places).astype(

time: 435 us -> 528 us (1.21)
  the two profiles are of different devices: /device:TPU:16 before, /device:TPU:4 now
where the time goes in v1:
time: 528 us; the launch traced here: 523 us
  waiting for transfers between devices  256 us (48%)
  matrix products  85.6 us (16%)
  local copies, waits for them, and re-layouts  69 us (13%)
  other arithmetic  41.6 us (8%)
  blocking collectives  37.4 us (7%)
  starting transfers between devices  19.5 us (4%)
  between operations  14.1 us (3%)
    all_to_all x1, waiting for transfers between devices, on_device(): lax.all_to_all(jnp.stack([adapters] * lax.axis_size('exp')), 'exp', 0, 0)  105 us
    reduce_scatter x1, waiting for transfers between devices, on_device(): lax.psum_scatter(jnp.dot(flat_mixed, flat_out, preferred_element_type=jnp...  83.5 us
    all_gather x1, waiting for transfers between devices, on_device(): lax.all_gather(normed, 'exp', axis=0, tiled=True)  42.1 us
    all_to_all x1, blocking collectives, on_device(): lax.all_to_all(spread_rows, 'exp', split_axis=0, concat_axis=0, tiled=True)  37.4 us
    all_to_all x1, waiting for transfers between devices, on_device(): lax.all_to_all(partial_out.astype(jnp.bfloat16), 'exp', split_axis=0, con...  25.1 us
    dot_general x4, matrix products, attend_block(): jnp.einsum('qhd,khd->hqk', queries, key_rows, preferred_element_type=jnp....  16 us
    dot_general x1, matrix products, on_device(): jnp.einsum('tje,tjx->tex', slot_weights, heads_out.astype(jnp.float32), p...  14.3 us
    gather x1, local copies, waits for them, and re-layouts, on_device(): jnp.take(queries.reshape(group_rows * AEXP, local_heads * HD), chosen_row...  12.9 us
  transfers between devices with their start and end apart: 5, of which 4 were waited for; matrix products, arithmetic and copies ran while one was open for 11% of the time, Pallas kernels for 0%

profile of v1, /device:TPU:4, one launch (start us, length us, event | category | flops | bytes accessed | tf_op | source)
XLA Modules:
  0.0 523.3 jit_solution(15234287241469977093)
XLA Ops:
  13.8 4.9 all-to-all-start
  23.8 3.3 copy.159
  27.1 4.3 copy.123
  42.6 42.1 %all-gather.2.cloned.1.call-done = bf16[2048,2048]{1,0:T(8,128)(2,1)} async-done(((bf16[128,2048]{1,0:T(8,128)(2,1)}), bf16[2048,2048]{1,0:T(8,128)(2,1)}) %all-gather.2.cloned.1.call-update) | async-done | bytes 8388624 | tf_op jit(solution)/shard_map/all_gather | solution.py:109
  84.8 5.9 %fusion.24 = f32[2048,2,1,128]{0,3,1,2:T(8,128)S(1)} fusion(bf16[2,128,2048]{2,1,0:T(8,128)(2,1)S(1)} %bitcast.179, bf16[2048,2048]{1,0:T(8,128)(2,1)} %all-gather.2.cloned.1.call-done), kind=kOutput, calls=%fused_computation.34 | convolution fusion | flops 2147483648 | bytes 11534336 | tf_op jit(solution)/shard_map/dot_general | solution.py:120
  92.6 4.5 fusion.18
  98.9 4.1 copy.125
  105.4 4.3 fusion.49
  112.1 4.7 pad_maximum_fusion
  116.8 12.9 %gather_fusion = bf16[4096,128]{1,0:T(8,128)(2,1)S(1)} fusion(bf16[8192,128]{1,0:T(8,128)(2,1)} %pad_maximum_fusion, s32[4096]{0:T(1024)S(1)} %copy-done.15), kind=kCustom, calls=%fused_computation | custom fusion | bytes 2113536 | tf_op jit(solution)/shard_map/jit(_take)/gather | solution.py:119
  131.9 37.0 %while.11 = (s32[]{:T(128)}, bf16[4,1024,1,128]{3,1,2,0:T(8,128)(2,1)}, s32[4,1024]{1,0:T(4,128)}, s32[2560]{0:T(1024)S(1)}, s32[4,1024]{1,0:T(4,128)S(1)}, /*in...) while((s32[]{:T(128)}, ...), condition=%wide.region_8.9_spmd, body=%wide.region_5.8_spmd.sunk | while | flops 1371142144 | bytes 35979412 | solution.py:148
  132.7 4.0 fusion.96
  141.9 4.0 fusion.96
  151.1 4.0 fusion.96
  160.4 4.0 fusion.96
  168.8 14.3 %fusion.31 = bf16[2048,4,128]{2,1,0:T(4,128)(2,1)S(1)} fusion(bf16[2048,2,128]{2,1,0:T(2,128)(2,1)} %bitcast.196, f32[2048,2]{1,0:T(8,128)} %copy.120, s32[2048,2]{1,0:T(8,128)S(1)} %copy-done.7), kind=kOutput, calls=%fused_computation.46 | convolution fusion | flops 26247168 | bytes 3178496 | tf_op jit(solution)/shard_map/tje,tjx->tex/dot_general | solution.py:158
  183.2 6.6 %bitcast_convert_fusion = bf16[2048,2048]{1,0:T(8,128)(2,1)} fusion(bf16[4,128,2048]{2,1,0:T(8,128)(2,1)S(1)} %copy-done, bf16[2048,4,128]{2,1,0:T(4,128)(2,1)S(1)} %fusion.31), kind=kOutput, calls=%fused_computation.20 | convolution fusion | flops 4299161600 | bytes 12582912 | tf_op jit(solution)/shard_map/dot_general | solution.py:164
  192.0 83.5 %reduce-scatter.2.cloned.1.call-done = bf16[128,2048]{1,0:T(8,128)(2,1)} async-done(((bf16[2048,2048]{1,0:T(8,128)(2,1)}), bf16[128,2048]{1,0:T(8,128)(2,1)}) %reduce-scatter.2.cloned.1.call-update) | async-done | bytes 524304 | tf_op jit(solution)/shard_map/reduce_scatter | solution.py:163
  278.8 37.4 %all_to_all.20 = bf16[16,40,2048]{2,1,0:T(8,128)(2,1)} all-to-all(bf16[16,40,2048]{2,1,0:T(8,128)(2,1)S(1)} %bitcast.163), channel_id=1, replica_groups=mesh['req'=8,'exp'=16] {'exp'}, dimensions={0} | all-to-all | bytes 5242880 | tf_op jit(solution)/shard_map/all_to_all | solution.py:186
  316.2 4.3 stack.2
  320.5 5.0 all-to-all-start.3
  325.5 12.8 %fusion.10 = f32[640,2,1408]{2,0,1:T(8,128)S(1)} fusion(bf16[640,2048,1]{1,0,2:T(8,128)(2,1)} %bitcast.172, bf16[2048,2,1408]{2,1,0:T(2,128)(2,1)} %param.28), kind=kOutput, calls=%fused_computation.21 | convolution fusion | flops 7381975040 | bytes 21364736 | tf_op jit(solution)/shard_map/nd,dkf->nkf/dot_general | solution.py:188
  338.8 8.5 %fusion.21 = bf16[16,40,2048]{2,1,0:T(8,128)(2,1)} fusion(bf16[1408,2048]{1,0:T(8,128)(2,1)} %param.29, f32[16,40,1408]{2,1,0:T(8,128)S(1)} %bitcast.171, f32[16,40,1408]{2,1,0:T(8,128)S(1)} %bitcast.170), kind=kOutput, calls=%fused_computation.33 | convolution fusion | flops 3697704960 | bytes 15597568 | tf_op jit(solution)/shard_map/dot_general | solution.py:190
  347.3 105.4 %all-to-all-done.3 = bf16[16,4,2,16,2048]{4,3,2,1,0:T(8,128)(2,1)} async-done(((bf16[16,4,2,16,2048]{4,3,2,1,0:T(8,128)(2,1)}), bf16[16,4,2,16,2048]{4,3,2,1,0:T(8,128)(2,1)}, u32[]{:S(2)}, u32[]{:S(2)}) %all-to-all-start.3) | async-done | bytes 8388640 | tf_op jit(solution)/shard_map/all_to_all | solution.py:111
  452.7 9.6 %all-to-all-start.2 = ((bf16[16,40,2048]{2,1,0:T(8,128)(2,1)}), bf16[16,40,2048]{2,1,0:T(8,128)(2,1)}, u32[]{:S(2)}, u32[]{:S(2)}) async-start(bf16[16,40,2048]{2,1,0:T(8,128)(2,1)} %fusion.21), calls=%async_computation.3 | async-start | bytes 5242880 | tf_op jit(solution)/shard_map/all_to_all | solution.py:193
  463.6 4.0 gather_fusion.2
  468.5 25.1 %all-to-all-done.2 = bf16[16,40,2048]{2,1,0:T(8,128)(2,1)} async-done(((bf16[16,40,2048]{2,1,0:T(8,128)(2,1)}), bf16[16,40,2048]{2,1,0:T(8,128)(2,1)}, u32[]{:S(2)}, u32[]{:S(2)}) %all-to-all-start.2) | async-done | bytes 2621472 | tf_op jit(solution)/shard_map/all_to_all | solution.py:193
  493.6 4.1 convert_reduce_fusion
  497.7 5.4 %gather_fusion.1 = f32[256,2048]{1,0:T(8,128)} fusion(f32[320,2048]{1,0:T(8,128)} %bitcast.162, s32[1024]{0:T(1024)S(1)} %pad_clamp_fusion.1), kind=kCustom, calls=%fused_computation.1 | custom fusion | bytes 4195328 | tf_op jit(solution)/shard_map/jit(_take)/gather | solution.py:199
  503.0 3.5 gather.19
  506.5 6.6 %multiply_reduce_fusion = f32[128,2048]{1,0:T(8,128)} fusion(f32[128,2,2048]{2,1,0:T(2,128)} %gather.19, pred[128,2]{1,0:T(8,128)(4,1)S(1)} %copy.139, f32[128,2]{1,0:T(8,128)S(1)} %copy.142), kind=kLoop, calls=%fused_computation.42 | loop fusion | flops 1310720 | bytes 3147008 | tf_op jit(solution)/shard_map/reduce_sum | solution.py:200
  513.1 3.1 fusion.28
  (161 shorter events, 63.1 us)
Async XLA Ops:
  6.5 176.6 %copy-start = (bf16[4,128,2048]{2,1,0:T(8,128)(2,1)S(1)}, bf16[4,128,2048]{2,1,0:T(8,128)(2,1)}, u32[]{:S(2)}) copy-start(bf16[4,128,2048]{2,1,0:T(8,128)(2,1)} %param.22) | copy-start | bytes 6291460
  6.5 6.0 %copy-start.24 = (s32[32]{0:T(128)S(1)}, s32[32]{0:T(128)}, u32[]{:S(2)}) copy-start(s32[32]{0:T(128)} %param.24) | copy-start | bytes 388
  6.5 78.2 %all-gather.2.cloned.1.call-start = ((), (), s32[]{:S(2)}) async-start(), calls=%async_computation.5 | async-start | bytes 8912896 | tf_op jit(solution)/shard_map/all_gather | solution.py:109
  9.3 9.5 %copy-start.14 = (s32[2048,2]{0,1:T(2,128)S(1)}, s32[2048,2]{0,1:T(2,128)}, u32[]{:S(2)}) copy-start(s32[2048,2]{0,1:T(2,128)} %param.26) | copy-start | bytes 49156
  13.8 7.9 %copy-start.25 = (s32[1,4]{1,0:T(1,128)S(1)}, s32[1,4]{1,0:T(1,128)}, u32[]{:S(2)}) copy-start(s32[1,4]{1,0:T(1,128)} %param.25) | copy-start | bytes 52
  13.8 26.8 %all-to-all-start = ((bf16[8,128,1,256]{3,1,2,0:T(8,128)(2,1)}), bf16[8,128,1,256]{3,1,2,0:T(8,128)(2,1)}, u32[]{:S(2)}, u32[]{:S(2)}) async-start(bf16[8,128,1,256]{3,1,2,0:T(8,128)(2,1)} %copy.128), calls=%async_computation | async-start | bytes 1048576 | tf_op jit(solution)/shard_map/all_to_all | solution.py:96
  18.8 256.8 %reduce-scatter.2.cloned.1.call-start = ((), (), s32[]{:S(2)}) async-start(), calls=%async_computation.6 | async-start | bytes 8912896 | tf_op jit(solution)/shard_map/reduce_scatter | solution.py:163
  22.0 14.4 %copy-start.11 = (s32[2048]{0:T(1024)}, s32[2048]{0:T(1024)S(1)}, u32[]{:S(2)}) copy-start(s32[2048]{0:T(1024)S(1)} %convert_reduce_fusion.1) | copy-start | bytes 24580
  31.4 2.8 copy-start.16
  34.2 50.5 %copy-start.8 = (bf16[256,2048]{1,0:T(8,128)(2,1)S(1)}, bf16[256,2048]{1,0:T(8,128)(2,1)}, u32[]{:S(2)}) copy-start(bf16[256,2048]{1,0:T(8,128)(2,1)} %copy.130) | copy-start | bytes 3145732
  35.6 6.7 %copy-start.20 = (f32[64]{0:T(128)}, f32[64]{0:T(128)S(1)}, u32[]{:S(2)}) copy-start(f32[64]{0:T(128)S(1)} %multiply_power_fusion) | copy-start | bytes 772
  36.5 5.8 %copy-start.12 = (f32[2048]{0:T(1024)}, f32[2048]{0:T(1024)S(1)}, u32[]{:S(2)}) copy-start(f32[2048]{0:T(1024)S(1)} %subtract_convert_fusion.1) | copy-start | bytes 24580
  84.8 7.8 %copy-start.23 = (bf16[2048,2048]{1,0:T(8,128)(2,1)S(1)}, bf16[2048,2048]{1,0:T(8,128)(2,1)}, u32[]{:S(2)}) copy-start(bf16[2048,2048]{1,0:T(8,128)(2,1)} %all-gather.2.cloned.1.call-done) | copy-start | bytes 25165828
  90.7 2.0 copy-start.5
  92.6 4.5 copy-start.3
  92.6 4.5 copy-start.4
  105.4 5.5 %copy-start.6 = (bf16[2048,1,128]{0,2,1:T(8,128)(2,1)S(1)}, bf16[2048,1,128]{0,2,1:T(8,128)(2,1)}, u32[]{:S(2)}) copy-start(bf16[2048,1,128]{0,2,1:T(8,128)(2,1)} %fusion.52) | copy-start | bytes 1572868
  112.1 4.7 copy-start.15
  116.8 13.0 %copy-start.17 = (pred[4,1024]{1,0:T(4,128)(4,1)S(1)}, pred[4,1024]{1,0:T(4,128)(4,1)}, u32[]{:S(2)}) copy-start(pred[4,1024]{1,0:T(4,128)(4,1)} %compare_and_fusion) | copy-start | bytes 12292
  116.8 15.1 %copy-start.18 = (s32[2560]{0:T(1024)S(1)}, s32[2560]{0:T(1024)}, u32[]{:S(2)}) copy-start(s32[2560]{0:T(1024)} %pad_add_fusion) | copy-start | bytes 30724
  116.8 15.1 %copy-start.26 = (s32[2560]{0:T(1024)S(1)}, s32[2560]{0:T(1024)}, u32[]{:S(2)}) copy-start(s32[2560]{0:T(1024)} %constant.115.clone.1) | copy-start | bytes 30724
  131.9 37.0 %copy-start.7 = (s32[2048,2]{1,0:T(8,128)S(1)}, s32[2048,2]{1,0:T(8,128)}, u32[]{:S(2)}) copy-start(s32[2048,2]{1,0:T(8,128)} %copy.119) | copy-start | bytes 49156
  136.7 1.6 copy-start.9
  145.9 1.6 copy-start.9
  189.7 85.8 %copy-start.1 = (bf16[128,2048]{1,0:T(8,128)(2,1)S(1)}, bf16[128,2048]{1,0:T(8,128)(2,1)}, u32[]{:S(2)}) copy-start(bf16[128,2048]{1,0:T(8,128)(2,1)} %param.18) | copy-start | bytes 1572868
  189.7 87.1 %copy-start.13 = (f32[1,2048]{1,0:T(1,128)S(1)}, f32[1,2048]{1,0:T(1,128)}, u32[]{:S(2)}) copy-start(f32[1,2048]{1,0:T(1,128)} %get-tuple-element.158) | copy-start | bytes 24580
  278.8 37.4 %copy-start.10 = (bf16[4,2,16,2048]{3,2,1,0:T(8,128)(2,1)S(1)}, bf16[4,2,16,2048]{3,2,1,0:T(8,128)(2,1)}, u32[]{:S(2)}) copy-start(bf16[4,2,16,2048]{3,2,1,0:T(8,128)(2,1)} %param.32) | copy-start | bytes 1572868
  320.5 132.1 %all-to-all-start.3 = ((bf16[16,4,2,16,2048]{4,3,2,1,0:T(8,128)(2,1)}), bf16[16,4,2,16,2048]{4,3,2,1,0:T(8,128)(2,1)}, u32[]{:S(2)}, u32[]{:S(2)}) async-start(bf16[16,4,2,16,2048]{4,3,2,1,0:T(8,128)(2,1)} %stack.2), calls=%async_computation.4 | async-start | bytes 16777216 | tf_op jit(solution)/shard_map/all_to_all | solution.py:111
  347.3 115.3 %copy-start.21 = (f32[128,2]{0,1:T(2,128)S(1)}, f32[128,2]{0,1:T(2,128)}, u32[]{:S(2)}) copy-start(f32[128,2]{0,1:T(2,128)} %param.31) | copy-start | bytes 3076
  347.3 116.2 %copy-start.22 = (s32[32]{0:T(128)S(1)}, s32[32]{0:T(128)}, u32[]{:S(2)}) copy-start(s32[32]{0:T(128)} %param.33) | copy-start | bytes 388
  452.7 40.9 %all-to-all-start.2 = ((bf16[16,40,2048]{2,1,0:T(8,128)(2,1)}), bf16[16,40,2048]{2,1,0:T(8,128)(2,1)}, u32[]{:S(2)}, u32[]{:S(2)}) async-start(bf16[16,40,2048]{2,1,0:T(8,128)(2,1)} %fusion.21), calls=%async_computation.3 | async-start | bytes 5242880 | tf_op jit(solution)/shard_map/all_to_all | solution.py:193
  506.5 6.6 %copy-start.2 = (bf16[128,2048]{1,0:T(8,128)(2,1)S(1)}, bf16[128,2048]{1,0:T(8,128)(2,1)}, u32[]{:S(2)}) copy-start(bf16[128,2048]{1,0:T(8,128)(2,1)} %reduce-scatter.2.cloned.1.call-done) | copy-start | bytes 1572868
  (3 other events, 3.8 us)
Sparse Core Ops, SparseCore 0:
  11.5 73.2 all-gather.1
  189.9 85.6 reduce-scatter.1
